TPU v7x, 32 devices: a whole 2x2x4 slice. The times are simulated.
32 devices in a mesh: dp: 4 (over y, core), expert: 4 (over z), tensor: 2 (over x).
Axes of the slice: x: 2, y: 2, z: 4, core: 2. Of those that a mesh axis runs over, the one named last changes fastest.
Arguments:
- grad_out: bfloat16 [4096, 2048], P(('dp', 'expert', 'tensor')), may hold values from -6 to 6
- expert_ids: int32 [4096, 2], P(('dp', 'expert', 'tensor')), may hold values from 0 to 63, all different within a row; in each aligned block of 128 rows (0 to 127, 128 to 255, ...) at most 5 rows name the same one
- gate_weights: float32 [4096, 2], P(('dp', 'expert', 'tensor')), may hold values from 0.05 to 0.6
- overflow: int32 [4096, 2], P(('dp', 'expert', 'tensor')), may hold values 0 or 1
- saved_gate: bfloat16 [64, 4, 8, 5, 1408], P(('expert', 'tensor'), None, None, None, 'dp'), may hold values from -6 to 6
- saved_up: bfloat16 [64, 4, 8, 5, 1408], P(('expert', 'tensor'), None, None, None, 'dp'), may hold values from -6 to 6
- w_gate: bfloat16 [64, 2048, 1408], P(('expert', 'tensor'), None, 'dp'), may hold values from -0.125 to 0.125
- w_up: bfloat16 [64, 2048, 1408], P(('expert', 'tensor'), None, 'dp'), may hold values from -0.125 to 0.125
- w_down: bfloat16 [64, 1408, 2048], P(('expert', 'tensor'), 'dp'), may hold values from -0.15625 to 0.15625
- shared_gate_act: bfloat16 [4096, 1408], P(('dp', 'expert'), 'tensor'), may hold values from -6 to 6
- shared_up_act: bfloat16 [4096, 1408], P(('dp', 'expert'), 'tensor'), may hold values from -6 to 6
- ws_gate: bfloat16 [2048, 1408], P(None, 'tensor'), may hold values from -0.125 to 0.125
- ws_up: bfloat16 [2048, 1408], P(None, 'tensor'), may hold values from -0.125 to 0.125
- ws_down: bfloat16 [1408, 2048], P('tensor'), may hold values from -0.15625 to 0.15625
- w_out: bfloat16 [2048, 2048], P('tensor'), may hold values from -0.125 to 0.125
Outputs:
- grad_hidden: bfloat16 [4096, 2048], P(('dp', 'expert', 'tensor'))
- grad_context: bfloat16 [4096, 2048], P(('dp', 'expert'), 'tensor')
Inputs may be any that keep to these rules, and one draw needn't show every extreme that they name: `expert_ids`: each row names 2 different experts; within the rows of one device (aligned blocks of 128 rows) no expert is named by more than 5 rows, a bound that some block reaches.
All inputs are finite; a program needn't handle non-finite values. No bound on the sum of `overflow` on one device may be relied on, other than what follows from the above.
Results may differ from a plain program's by a relative error of at most 0.015.
Values may be sent and summed in bfloat16 or wider, within the bound.
No kernel may reach another device: no remote copies, remote signals or barrier semaphores. Data moves between devices by JAX's collectives and lax.ppermute only.
A program may use at most 128 MiB of HBM per device.

v0:
```python
import jax
import jax.numpy as jnp
from jax import lax
from jax.sharding import PartitionSpec as P


def rank_in_block(pair_experts, expert_total):
    onehot = (pair_experts[:, None] == jnp.arange(expert_total, dtype=jnp.int32)[None, :]).astype(
        jnp.int32
    )
    earlier = jnp.cumsum(onehot, axis=0) - onehot
    return jnp.sum(earlier * onehot, axis=1)


def fill_slots(pair_grads, pair_experts, expert_total, capacity):
    pair_count, model_width = pair_grads.shape
    destination = pair_experts * capacity + rank_in_block(pair_experts, expert_total)
    source = jnp.full((expert_total * capacity,), pair_count, jnp.int32)
    source = source.at[destination].set(jnp.arange(pair_count, dtype=jnp.int32))
    padded = jnp.concatenate([pair_grads, jnp.zeros((1, model_width), pair_grads.dtype)], axis=0)
    return (padded[source].reshape(expert_total, capacity, model_width), destination)


def weighted_pairs(grads, weights):
    scaled = grads.astype(jnp.float32)[:, None, :] * weights.astype(jnp.float32)[:, :, None]
    return scaled.astype(jnp.bfloat16).reshape(-1, grads.shape[1])


def swiglu_backward(hidden_activation, gate_act, up_act):
    gate_value = gate_act.astype(jnp.float32)
    sigmoid_value = jax.nn.sigmoid(gate_value)
    gate_input_gradient = (
        hidden_activation
        * up_act.astype(jnp.float32)
        * sigmoid_value
        * (1.0 + gate_value * (1.0 - sigmoid_value))
    ).astype(jnp.bfloat16)
    up_input_gradient = (hidden_activation * gate_value * sigmoid_value).astype(jnp.bfloat16)
    return (gate_input_gradient, up_input_gradient)


def expert_terms(
    capacity_slot_rows,
    gate_act,
    up_act,
    gate_projection_weight,
    up_projection_weight,
    down_projection_weight,
):
    hidden_activation = jnp.einsum(
        "cyg,cog->cyo",
        capacity_slot_rows,
        down_projection_weight,
        preferred_element_type=jnp.float32,
    )
    gate_input_gradient, up_input_gradient = swiglu_backward(hidden_activation, gate_act, up_act)
    input_gradient_output = jnp.einsum(
        "etv,ebv->etb",
        gate_input_gradient,
        gate_projection_weight,
        preferred_element_type=jnp.float32,
    )
    input_gradient_output = input_gradient_output + jnp.einsum(
        "etv,ebv->etb", up_input_gradient, up_projection_weight, preferred_element_type=jnp.float32
    )
    return lax.optimization_barrier(input_gradient_output.astype(jnp.bfloat16))


def body(
    grad_out,
    expert_ids,
    gate_weights,
    overflow,
    saved_gate,
    saved_up,
    w_gate,
    w_up,
    w_down,
    shared_gate_act,
    shared_up_act,
    ws_gate,
    ws_up,
    ws_down,
    w_out,
):
    dp_count = lax.axis_size("dp")
    group_count = lax.axis_size(("expert", "tensor"))
    expert_local, unused_dp, unused_group, capacity, unit_part = saved_gate.shape
    expert_total = expert_local * group_count
    token_count, model_width = grad_out.shape
    top_count = expert_ids.shape[1]
    flag_values = overflow.astype(jnp.float32)
    routed_weight = (gate_weights * (1.0 - flag_values)).astype(jnp.bfloat16)
    shared_weight = 1.0 + jnp.sum(gate_weights * flag_values, axis=1)
    pair_grads = weighted_pairs(grad_out, routed_weight)
    filled, destination = fill_slots(pair_grads, expert_ids.reshape(-1), expert_total, capacity)
    arrived = lax.all_to_all(
        filled[:, None], ("expert", "tensor"), split_axis=0, concat_axis=1, tiled=True
    )
    everyone = lax.all_gather(arrived[:, None], "dp", axis=1, tiled=True)
    terms = expert_terms(
        everyone.reshape(expert_local, -1, model_width),
        saved_gate.reshape(expert_local, -1, unit_part),
        saved_up.reshape(expert_local, -1, unit_part),
        w_gate,
        w_up,
        w_down,
    )
    terms = terms.astype(jnp.float32).reshape(
        expert_local, dp_count, group_count, capacity, model_width
    )
    summed = lax.psum_scatter(
        terms.astype(jnp.bfloat16), "dp", scatter_dimension=1, tiled=True
    ).astype(jnp.float32)
    returned = lax.all_to_all(
        summed[:, 0].astype(jnp.bfloat16),
        ("expert", "tensor"),
        split_axis=1,
        concat_axis=0,
        tiled=True,
    ).astype(jnp.float32)
    picked = returned.reshape(expert_total * capacity, model_width)[destination]
    routed = jnp.sum(picked.reshape(token_count, top_count, model_width), axis=1)
    routed_total = routed.astype(jnp.bfloat16)
    shared_grad = (grad_out.astype(jnp.float32) * shared_weight[:, None]).astype(jnp.bfloat16)
    group_shared = lax.all_gather(shared_grad, "tensor", axis=0, tiled=True)
    shared_hidden = jnp.einsum(
        "td,fd->tf", group_shared, ws_down, preferred_element_type=jnp.float32
    )
    shared_gate_grad, shared_up_grad = swiglu_backward(
        shared_hidden, shared_gate_act, shared_up_act
    )
    partial_value = jnp.einsum(
        "tf,df->td", shared_gate_grad, ws_gate, preferred_element_type=jnp.float32
    )
    partial_value = partial_value + jnp.einsum(
        "tf,df->td", shared_up_grad, ws_up, preferred_element_type=jnp.float32
    )
    partial_value = lax.optimization_barrier(partial_value.astype(jnp.bfloat16)).astype(jnp.float32)
    own_shared = lax.psum_scatter(
        partial_value.astype(jnp.bfloat16), "tensor", scatter_dimension=0, tiled=True
    ).astype(jnp.float32)
    grad_hidden = (
        grad_out.astype(jnp.float32) + own_shared + routed_total.astype(jnp.float32)
    ).astype(jnp.bfloat16)
    grad_group = lax.all_gather(grad_hidden, "tensor", axis=0, tiled=True)
    grad_context = jnp.einsum(
        "td,hd->th", grad_group, w_out, preferred_element_type=jnp.float32
    ).astype(jnp.bfloat16)
    return (grad_hidden, grad_context)


def solution(mesh):
    in_specs = (
        P(("dp", "expert", "tensor"), None),
        P(("dp", "expert", "tensor"), None),
        P(("dp", "expert", "tensor"), None),
        P(("dp", "expert", "tensor"), None),
        P(("expert", "tensor"), None, None, None, "dp"),
        P(("expert", "tensor"), None, None, None, "dp"),
        P(("expert", "tensor"), None, "dp"),
        P(("expert", "tensor"), None, "dp"),
        P(("expert", "tensor"), "dp", None),
        P(("dp", "expert"), "tensor"),
        P(("dp", "expert"), "tensor"),
        P(None, "tensor"),
        P(None, "tensor"),
        P("tensor", None),
        P("tensor", None),
    )
    out_specs = (P(("dp", "expert", "tensor"), None), P(("dp", "expert"), "tensor"))
    return jax.shard_map(body, mesh=mesh, in_specs=in_specs, out_specs=out_specs, check_vma=False)
```

profile of v0, /device:TPU:0, one launch (start us, length us, event | category | flops | bytes accessed | tf_op | source)
XLA Modules:
  0.0 329.5 jit_solution(9769154388567705892)
XLA Ops:
  7.2 0.0 copy-start
  7.2 0.0 all-gather.9.cloned.1.call-start
  7.2 0.9 copy.38
  8.2 0.1 eq.29
  8.3 0.1 eq.25
  8.4 0.7 broadcast_multiply_fusion
  9.1 0.6 reduce-window.6
  9.8 0.2 slice_reduce_fusion
  10.0 0.1 copy.37
  10.1 0.1 mul.107
  10.2 0.1 fusion.25
  10.4 1.4 scatter_custom_fusion
  11.8 0.7 fusion.29
  12.5 0.1 copy.36
  12.6 0.1 reshape.88
  12.8 3.4 %mul.98 = f32[128,2,2048]{2,1,0:T(2,128)} broadcast(bf16[128,2048]{1,0:T(8,128)(2,1)} %param.15), dimensions={0,2} | broadcast | bytes 2621440 | tf_op jit(solution)/shard_map/mul | solution.py:25
  16.2 3.7 %mul.99 = f32[256,2048]{1,0:T(8,128)} reshape(f32[128,2,2048]{2,1,0:T(2,128)} %mul.98) | data formatting | bytes 4194304 | tf_op jit(solution)/shard_map/mul | solution.py:25
  19.9 1.8 multiply_convert_fusion
  21.6 1.1 concatenate.3
  22.7 6.3 %gather_fusion = bf16[320,2048]{1,0:T(8,128)(2,1)} fusion(bf16[257,2048]{1,0:T(8,128)(2,1)} %concatenate.3, s32[1024]{0:T(1024)S(1)} %pad_clamp_fusion.1), kind=kCustom, calls=%fused_computation | custom fusion | bytes 2622720 | tf_op jit(solution)/shard_map/gather | solution.py:21
  29.1 3.4 %broadcast_in_dim_reshape.4 = bf16[64,1,5,2048]{3,2,0,1:T(8,128)(2,1)} reshape(bf16[320,2048]{1,0:T(8,128)(2,1)} %gather_fusion) | data formatting | bytes 2621440 | tf_op jit(solution)/shard_map/broadcast_in_dim;reshape | solution.py:98
  32.5 55.5 %all_to_all.24 = bf16[64,1,5,2048]{3,2,1,0:T(8,128)(2,1)S(1)} all-to-all(bf16[64,1,5,2048]{3,2,1,0:T(8,128)(2,1)} %bitcast.53), channel_id=1, replica_groups=mesh['dp'=4,'expert'=4,'tensor'=2] {'expert','tensor'}, dimensions={0} | all-to-all | bytes 2621440 | tf_op jit(solution)/shard_map/all_to_all | solution.py:97
  88.0 2.0 copy.70
  89.9 0.0 all-gather.9.cloned.1.call-update
  90.0 0.0 all-gather.5.cloned.1.call-start
  90.0 0.0 copy-done.2
  90.0 0.9 multiply_convert_fusion.2
  91.0 0.0 all-gather.5.cloned.1.call-update
  91.0 0.5 reduce-scatter.5.cloned.1.call-start
  91.5 0.0 copy-start.5
  91.5 1.6 copy.47
  93.2 1.6 bitcast_convert_fusion.1
  94.7 0.3 copy.45
  95.0 1.5 bitcast_convert_fusion
  96.5 33.0 %all-gather.9.cloned.1.call-done = bf16[8,32,1,5,2048]{4,0,1,3,2:T(8,128)(2,1)} async-done(((bf16[8,8,1,5,2048]{4,0,1,3,2:T(8,128)(2,1)}), bf16[8,32,1,5,2048]{4,0,1,3,2:T(8,128)(2,1)}) %all-gather.9.cloned.1.call-update) | async-done | bytes 5242896 | tf_op jit(solution)/shard_map/all_gather | solution.py:100
  129.6 5.7 %copy.43 = bf16[8,32,1,5,2048]{4,0,3,1,2:T(8,128)(2,1)} copy(bf16[8,32,1,5,2048]{4,0,1,3,2:T(8,128)(2,1)} %all-gather.9.cloned.1.call-done) | data formatting | bytes 10485760 | tf_op jit(solution)/shard_map/all_gather | solution.py:100
  135.3 15.0 %fusion = f32[8,160,352]{2,1,0:T(8,128)} fusion(bf16[8,352,2048]{2,1,0:T(8,128)(2,1)} %param.23, bf16[8,160,2048]{2,0,1:T(8,128)(2,1)} %bitcast.54), kind=kOutput, calls=%fused_computation.4 | convolution fusion | flops 1845493760 | bytes 18579456 | tf_op jit(solution)/shard_map/cyg,cog->cyo/dot_general | solution.py:50
  150.2 13.2 %fusion.6 = f32[8,160,2048]{2,1,0:T(8,128)} fusion(bf16[8,2048,352]{1,2,0:T(8,128)(2,1)} %param.21, f32[8,160,352]{2,1,0:T(8,128)} %fusion, f32[8,160,352]{2,0,1:T(8,128)} %bitcast_convert_fusion, f32[8,160,352]{2,0,1:T(8,128)S(1)} %copy-done.1), kind=kOutput, calls=%fused_computation.23 | convolution fusion | flops 1849999360 | bytes 27426816 | tf_op jit(solution)/shard_map/etv,ebv->etb/dot_general | solution.py:57
  163.4 13.3 %add_convert_fusion = bf16[8,160,2048]{2,1,0:T(8,128)(2,1)} fusion(f32[8,160,2048]{2,1,0:T(8,128)} %fusion.6, bf16[8,2048,352]{1,2,0:T(8,128)(2,1)} %param.22, f32[8,160,352]{2,1,0:T(8,128)} %fusion, f32[8,160,352]{2,0,1:T(8,128)S(1)} %copy-done.1), kind=kOutput, calls=%fused_computation.3 | convolution fusion | flops 1853440000 | bytes 30867456 | tf_op jit(solution)/shard_map/etv,ebv->etb/dot_general | solution.py:63
  176.8 7.7 %copy.51 = bf16[8,160,2048]{2,0,1:T(8,128)(2,1)} copy(bf16[8,160,2048]{2,1,0:T(8,128)(2,1)} %add_convert_fusion) | data formatting | bytes 10485760 | tf_op jit(solution)/shard_map/optimization_barrier | solution.py:66
  184.4 0.0 reduce-scatter.5.cloned.1.call-update
  184.4 0.0 all-gather.5.cloned.1.call-done
  184.5 4.0 %fusion.34 = f32[256,704]{0,1:T(8,128)} fusion(bf16[256,2048]{1,0:T(8,128)(2,1)} %all-gather.5.cloned.1.call-done, bf16[704,2048]{1,0:T(8,128)(2,1)} %param.28), kind=kOutput, calls=%fused_computation.63 | convolution fusion | flops 738197504 | bytes 4653056 | tf_op jit(solution)/shard_map/td,fd->tf/dot_general | solution.py:127
  188.5 47.5 %reduce-scatter.5.cloned.1.call-done = bf16[8,1,8,5,2048]{4,0,3,2,1:T(8,128)(2,1)} async-done(((bf16[8,4,8,5,2048]{4,0,3,2,1:T(8,128)(2,1)}), bf16[8,1,8,5,2048]{4,0,3,2,1:T(8,128)(2,1)}) %reduce-scatter.5.cloned.1.call-update) | async-done | bytes 1310736 | tf_op jit(solution)/shard_map/reduce_scatter | solution.py:112
  236.0 5.5 %all-to-all-start.1 = ((bf16[8,8,5,2048]{3,0,2,1:T(8,128)(2,1)}), bf16[8,8,5,2048]{3,0,2,1:T(8,128)(2,1)}, u32[]{:S(2)}, u32[]{:S(2)}) async-start(bf16[8,8,5,2048]{3,0,2,1:T(8,128)(2,1)} %bitcast.56), calls=%async_computation.3 | async-start | bytes 2621440 | tf_op jit(solution)/shard_map/all_to_all | solution.py:115
  241.5 0.0 reduce-scatter.3.cloned.1.call-start
  241.5 0.0 copy-start.4
  241.6 0.0 copy-start.6
  241.6 2.5 fusion.19
  244.1 2.0 fusion.2
  246.1 0.0 reduce-scatter.3.cloned.1.call-update
  246.1 0.3 all-gather.7.cloned.1.call-start
  246.4 26.4 %all-to-all-done.1 = bf16[8,8,5,2048]{3,0,2,1:T(8,128)(2,1)} async-done(((bf16[8,8,5,2048]{3,0,2,1:T(8,128)(2,1)}), bf16[8,8,5,2048]{3,0,2,1:T(8,128)(2,1)}, u32[]{:S(2)}, u32[]{:S(2)}) %all-to-all-start.1) | async-done | bytes 1310752 | tf_op jit(solution)/shard_map/all_to_all | solution.py:115
  272.8 1.6 convert_bitcast_fusion
  274.4 3.5 %copy.52 = f32[8,8,1,5,2048]{4,3,1,0,2:T(8,128)} copy(f32[8,8,1,5,2048]{4,1,3,0,2:T(8,128)S(1)} %convert_bitcast_fusion) | data formatting | bytes 5242880 | tf_op jit(solution)/shard_map/convert_element_type | solution.py:121
  277.9 4.6 %reshape.91 = f32[320,2048]{1,0:T(8,128)} reshape(f32[8,8,1,5,2048]{4,3,1,0,2:T(8,128)} %copy.52) | data formatting | bytes 5242880 | tf_op jit(solution)/shard_map/convert_element_type | solution.py:121
  282.5 5.4 %gather_fusion.1 = f32[256,2048]{1,0:T(8,128)} fusion(f32[320,2048]{1,0:T(8,128)} %reshape.91, s32[1024]{0:T(1024)S(1)} %pad_clamp_fusion), kind=kCustom, calls=%fused_computation.1 | custom fusion | bytes 4195328 | tf_op jit(solution)/shard_map/gather | solution.py:122
  287.8 3.5 %reshape.87 = f32[128,2,2048]{2,1,0:T(2,128)} reshape(f32[256,2048]{1,0:T(8,128)} %gather_fusion.1) | data formatting | bytes 4194304 | tf_op jit(solution)/shard_map/reshape | solution.py:123
  291.3 5.0 %reduce_sum.32 = bf16[128,2048]{1,0:T(8,128)(2,1)} reduce(f32[128,2,2048]{2,1,0:T(2,128)} %reshape.87, f32[]{:T(128)} %constant.8.clone.1), dimensions={1}, to_apply=%region_7.8 | reduce | flops 262144 | bytes 2621444 | tf_op jit(solution)/shard_map/reduce_sum | solution.py:123
  296.3 0.0 copy-done.3
  296.3 2.2 add_convert_fusion.1
  298.5 0.0 all-gather.7.cloned.1.call-update
  298.6 19.6 %all-gather.7.cloned.1.call-done = bf16[256,2048]{1,0:T(8,128)(2,1)} async-done(((bf16[128,2048]{1,0:T(8,128)(2,1)}), bf16[256,2048]{1,0:T(8,128)(2,1)}) %all-gather.7.cloned.1.call-update) | async-done | bytes 1048592 | tf_op jit(solution)/shard_map/all_gather | solution.py:146
  318.2 4.6 %convolution_convert_fusion = bf16[256,1024]{1,0:T(8,128)(2,1)} fusion(bf16[256,2048]{1,0:T(8,128)(2,1)} %all-gather.7.cloned.1.call-done, bf16[1024,2048]{1,0:T(8,128)(2,1)} %param.29), kind=kOutput, calls=%fused_computation.17 | convolution fusion | flops 1074003968 | bytes 5767168 | tf_op jit(solution)/shard_map/td,hd->th/dot_general | solution.py:147
  (20 shorter events, 0.1 us)
Async XLA Ops:
  7.2 234.4 %copy-start = (bf16[2048,704]{0,1:T(8,128)(2,1)S(1)}, bf16[2048,704]{0,1:T(8,128)(2,1)}, u32[]{:S(2)}) copy-start(bf16[2048,704]{0,1:T(8,128)(2,1)} %param.26) | copy-start | bytes 8650756
  7.2 122.4 %all-gather.9.cloned.1.call-start = ((), (), s32[]{:S(2)}) async-start(), calls=%async_computation.8 | async-start | bytes 6553600 | tf_op jit(solution)/shard_map/all_gather | solution.py:100
  88.0 2.1 copy-start.2
  90.0 94.5 %all-gather.5.cloned.1.call-start = ((), (), s32[]{:S(2)}) async-start(), calls=%async_computation.4 | async-start | bytes 1572864 | tf_op jit(solution)/shard_map/all_gather | solution.py:126
  91.0 145.0 %reduce-scatter.5.cloned.1.call-start = ((), (), s32[]{:S(2)}) async-start(), calls=%async_computation.6 | async-start | bytes 6553600 | tf_op jit(solution)/shard_map/reduce_scatter | solution.py:112
  91.5 3.2 copy-start.5
  135.3 15.0 %copy-start.1 = (f32[8,160,352]{2,0,1:T(8,128)S(1)}, f32[8,160,352]{2,0,1:T(8,128)}, u32[]{:S(2)}) copy-start(f32[8,160,352]{2,0,1:T(8,128)} %bitcast_convert_fusion.1) | copy-start | bytes 5406724
  188.5 53.1 %copy-start.7 = (bf16[256,704]{0,1:T(8,128)(2,1)S(1)}, bf16[256,704]{0,1:T(8,128)(2,1)}, u32[]{:S(2)}) copy-start(bf16[256,704]{0,1:T(8,128)(2,1)} %param.24) | copy-start | bytes 1081348
  236.0 36.8 %all-to-all-start.1 = ((bf16[8,8,5,2048]{3,0,2,1:T(8,128)(2,1)}), bf16[8,8,5,2048]{3,0,2,1:T(8,128)(2,1)}, u32[]{:S(2)}, u32[]{:S(2)}) async-start(bf16[8,8,5,2048]{3,0,2,1:T(8,128)(2,1)} %bitcast.56), calls=%async_computation.3 | async-start | bytes 2621440 | tf_op jit(solution)/shard_map/all_to_all | solution.py:115
  241.5 54.8 %reduce-scatter.3.cloned.1.call-start = ((), (), s32[]{:S(2)}) async-start(), calls=%async_computation.5 | async-start | bytes 1572864 | tf_op jit(solution)/shard_map/reduce_scatter | solution.py:140
  241.5 2.5 copy-start.4
  241.6 2.5 copy-start.6
  246.1 72.0 %all-gather.7.cloned.1.call-start = ((), (), s32[]{:S(2)}) async-start(), calls=%async_computation.7 | async-start | bytes 1572864 | tf_op jit(solution)/shard_map/all_gather | solution.py:146
  291.3 5.0 %copy-start.3 = (bf16[128,2048]{1,0:T(8,128)(2,1)S(1)}, bf16[128,2048]{1,0:T(8,128)(2,1)}, u32[]{:S(2)}) copy-start(bf16[128,2048]{1,0:T(8,128)(2,1)} %param.15) | copy-start | bytes 1572868
Sparse Core Ops, SparseCore 0:
  90.1 39.4 all-gather.8
  131.7 21.2 all-gather.4
  184.6 51.3 reduce-scatter.4
  246.3 26.1 reduce-scatter.2
  298.7 19.4 all-gather.6
where the time goes:
time: 336 us; the launch traced here: 330 us
  waiting for transfers between devices  127 us (38%)
  blocking collectives  55.5 us (17%)
  local copies, waits for them, and re-layouts  55.4 us (16%)
  matrix products  54.6 us (16%)
  other arithmetic  16.8 us (5%)
  between operations  14.2 us (4%)
  starting transfers between devices  6.39 us (2%)
    all_to_all x1, blocking collectives, body(): lax.all_to_all(filled[:, None], ('expert', 'tensor'), split_axis=0, conca...  55.5 us
    reduce_scatter x1, waiting for transfers between devices, body(): lax.psum_scatter(terms.astype(jnp.bfloat16), 'dp', scatter_dimension=1, t...  47.5 us
    all_gather x1, waiting for transfers between devices, body(): everyone = lax.all_gather(arrived[:, None], 'dp', axis=1, tiled=True)  33 us
    all_to_all x1, waiting for transfers between devices, body(): lax.all_to_all(summed[:, 0].astype(jnp.bfloat16), ('expert', 'tensor'), s...  26.4 us
    all_gather x1, waiting for transfers between devices, body(): grad_group = lax.all_gather(grad_hidden, 'tensor', axis=0, tiled=True)  19.6 us
    dot_general x1, matrix products, expert_terms(): jnp.einsum('cyg,cog->cyo', capacity_slot_rows, down_projection_weight, pr...  15 us
    dot_general x1, matrix products, expert_terms(): jnp.einsum('etv,ebv->etb', up_input_gradient, up_projection_weight, prefe...  13.3 us
    dot_general x1, matrix products, expert_terms(): jnp.einsum('etv,ebv->etb', gate_input_gradient, gate_projection_weight, p...  13.2 us
  transfers between devices with their start and end apart: 6, of which 4 were waited for; matrix products, arithmetic and copies ran while one was open for 28% of the time, Pallas kernels for 0%

commit v1 on v0

--- a/solution.py
+++ b/solution.py
@@ -2,6 +2,25 @@
 import jax.numpy as jnp
 from jax import lax
 from jax.sharding import PartitionSpec as P
+
+
+def joined_along(blocks, dim):
+    blocks = jnp.moveaxis(blocks, 0, dim)
+    shape = blocks.shape
+    return blocks.reshape(*shape[:dim], shape[dim] * shape[dim + 1], *shape[dim + 2 :])
+
+
+def work_around(value, axis, dim, work, out_dim):
+    length, mine, rows = (lax.axis_size(axis), lax.axis_index(axis), value.shape[dim])
+    right = [(i, (i + 1) % length) for i in range(length)]
+    tiles = []
+    carried = value
+    for hop in range(length):
+        coming = carried if hop == length - 1 else lax.ppermute(carried, axis, right)
+        tiles.append(work(carried, (mine - hop) % length * rows))
+        carried = coming
+    tiles = jnp.stack(tiles)[(mine - jnp.arange(length)) % length]
+    return joined_along(tiles, out_dim)
 
 
 def rank_in_block(pair_experts, expert_total):
@@ -143,9 +162,12 @@
     grad_hidden = (
         grad_out.astype(jnp.float32) + own_shared + routed_total.astype(jnp.float32)
     ).astype(jnp.bfloat16)
-    grad_group = lax.all_gather(grad_hidden, "tensor", axis=0, tiled=True)
-    grad_context = jnp.einsum(
-        "td,hd->th", grad_group, w_out, preferred_element_type=jnp.float32
+    grad_context = work_around(
+        grad_hidden,
+        "tensor",
+        0,
+        lambda part, at: jnp.einsum("td,hd->th", part, w_out, preferred_element_type=jnp.float32),
+        0,
     ).astype(jnp.bfloat16)
     return (grad_hidden, grad_context)
 

time: 336 us -> 326 us (0.970)
  waiting for transfers between devices: 127 us -> 114 us
    all_gather x1 -> x0, waiting for transfers between devices: 19.6 us -> none  [body(): grad_group = lax.all_gather(grad_hidden, 'tensor', axis=0, tiled=True)]
    ppermute x0 -> x1, waiting for transfers between devices: none -> 7.26 us  [work_around(): lax.ppermute(carried, axis, right)]
  transfers between devices with their start and end apart: 6 -> 6, of which waited for: 4 -> 4; matrix products, arithmetic and copies ran while one was open for 28% -> 30% of each run, Pallas kernels for 0% -> 0%
where the time goes in v1:
time: 326 us; the launch traced here: 320 us
  waiting for transfers between devices  114 us (35%)
  local copies, waits for them, and re-layouts  56.8 us (17%)
  blocking collectives  55.5 us (17%)
  matrix products  55.4 us (17%)
  other arithmetic  16.1 us (5%)
  between operations  14.2 us (4%)
  starting transfers between devices  7.87 us (2%)
    all_to_all x1, blocking collectives, body(): lax.all_to_all(filled[:, None], ('expert', 'tensor'), split_axis=0, conca...  55.5 us
    reduce_scatter x1, waiting for transfers between devices, body(): lax.psum_scatter(terms.astype(jnp.bfloat16), 'dp', scatter_dimension=1, t...  47.5 us
    all_gather x1, waiting for transfers between devices, body(): everyone = lax.all_gather(arrived[:, None], 'dp', axis=1, tiled=True)  33 us
    all_to_all x1, waiting for transfers between devices, body(): lax.all_to_all(summed[:, 0].astype(jnp.bfloat16), ('expert', 'tensor'), s...  26.4 us
    dot_general x1, matrix products, expert_terms(): jnp.einsum('cyg,cog->cyo', capacity_slot_rows, down_projection_weight, pr...  15 us
    dot_general x1, matrix products, expert_terms(): jnp.einsum('etv,ebv->etb', up_input_gradient, up_projection_weight, prefe...  13.3 us
    dot_general x1, matrix products, expert_terms(): jnp.einsum('etv,ebv->etb', gate_input_gradient, gate_projection_weight, p...  13.2 us
    convert_element_type x2, local copies, waits for them, and re-layouts, body(): returned = lax.all_to_all(summed[:, 0].astype(jnp.bfloat16), ('expert', '...  8.05 us
  transfers between devices with their start and end apart: 6, of which 4 were waited for; matrix products, arithmetic and copies ran while one was open for 30% of the time, Pallas kernels for 0%

profile of v1, /device:TPU:0, one launch (start us, length us, event | category | flops | bytes accessed | tf_op | source)
XLA Modules:
  0.0 320.2 jit_solution(1572355414896496289)
XLA Ops:
  7.2 0.0 copy-start
  7.2 0.0 all-gather.6.cloned.1.call-start
  7.2 0.9 copy.38
  8.2 0.1 eq.31
  8.3 0.1 eq.27
  8.4 0.7 broadcast_multiply_fusion
  9.1 0.6 reduce-window.6
  9.8 0.2 slice_reduce_fusion
  10.0 0.1 copy.37
  10.1 0.1 mul.107
  10.2 0.1 fusion.25
  10.4 1.4 scatter_custom_fusion
  11.8 0.7 fusion.29
  12.5 0.1 copy.36
  12.6 0.1 reshape.139
  12.8 3.4 %mul.98 = f32[128,2,2048]{2,1,0:T(2,128)} broadcast(bf16[128,2048]{1,0:T(8,128)(2,1)} %param.15), dimensions={0,2} | broadcast | bytes 2621440 | tf_op jit(solution)/shard_map/mul | solution.py:44
  16.2 3.7 %mul.99 = f32[256,2048]{1,0:T(8,128)} reshape(f32[128,2,2048]{2,1,0:T(2,128)} %mul.98) | data formatting | bytes 4194304 | tf_op jit(solution)/shard_map/mul | solution.py:44
  19.9 1.8 multiply_convert_fusion
  21.6 1.1 concatenate.3
  22.7 6.3 %gather_fusion = bf16[320,2048]{1,0:T(8,128)(2,1)} fusion(bf16[257,2048]{1,0:T(8,128)(2,1)} %concatenate.3, s32[1024]{0:T(1024)S(1)} %pad_clamp_fusion.2), kind=kCustom, calls=%fused_computation | custom fusion | bytes 2622720 | tf_op jit(solution)/shard_map/gather | solution.py:40
  29.1 3.4 %broadcast_in_dim_reshape.4 = bf16[64,1,5,2048]{3,2,0,1:T(8,128)(2,1)} reshape(bf16[320,2048]{1,0:T(8,128)(2,1)} %gather_fusion) | data formatting | bytes 2621440 | tf_op jit(solution)/shard_map/broadcast_in_dim;reshape | solution.py:117
  32.5 55.5 %all_to_all.24 = bf16[64,1,5,2048]{3,2,1,0:T(8,128)(2,1)S(1)} all-to-all(bf16[64,1,5,2048]{3,2,1,0:T(8,128)(2,1)} %bitcast.62), channel_id=1, replica_groups=mesh['dp'=4,'expert'=4,'tensor'=2] {'expert','tensor'}, dimensions={0} | all-to-all | bytes 2621440 | tf_op jit(solution)/shard_map/all_to_all | solution.py:116
  88.0 2.0 copy.70
  89.9 0.0 all-gather.6.cloned.1.call-update
  90.0 0.0 all-gather.4.cloned.1.call-start
  90.0 0.9 multiply_convert_fusion.2
  91.0 0.0 all-gather.4.cloned.1.call-update
  91.0 0.5 reduce-scatter.5.cloned.1.call-start
  91.5 0.0 copy-start.7
  91.5 1.6 copy.47
  93.2 1.6 bitcast_convert_fusion.1
  94.7 0.3 copy.45
  95.0 1.5 bitcast_convert_fusion
  96.5 33.0 %all-gather.6.cloned.1.call-done = bf16[8,32,1,5,2048]{4,0,1,3,2:T(8,128)(2,1)} async-done(((bf16[8,8,1,5,2048]{4,0,1,3,2:T(8,128)(2,1)}), bf16[8,32,1,5,2048]{4,0,1,3,2:T(8,128)(2,1)}) %all-gather.6.cloned.1.call-update) | async-done | bytes 5242896 | tf_op jit(solution)/shard_map/all_gather | solution.py:119
  129.6 5.7 %copy.43 = bf16[8,32,1,5,2048]{4,0,3,1,2:T(8,128)(2,1)} copy(bf16[8,32,1,5,2048]{4,0,1,3,2:T(8,128)(2,1)} %all-gather.6.cloned.1.call-done) | data formatting | bytes 10485760 | tf_op jit(solution)/shard_map/all_gather | solution.py:119
  135.3 15.0 %fusion = f32[8,160,352]{2,1,0:T(8,128)} fusion(bf16[8,352,2048]{2,1,0:T(8,128)(2,1)} %param.23, bf16[8,160,2048]{2,0,1:T(8,128)(2,1)} %bitcast.63), kind=kOutput, calls=%fused_computation.5 | convolution fusion | flops 1845493760 | bytes 18579456 | tf_op jit(solution)/shard_map/cyg,cog->cyo/dot_general | solution.py:69
  150.2 13.2 %fusion.6 = f32[8,160,2048]{2,1,0:T(8,128)} fusion(bf16[8,2048,352]{1,2,0:T(8,128)(2,1)} %param.21, f32[8,160,352]{2,1,0:T(8,128)} %fusion, f32[8,160,352]{2,0,1:T(8,128)} %bitcast_convert_fusion, f32[8,160,352]{2,0,1:T(8,128)S(1)} %copy-done.1), kind=kOutput, calls=%fused_computation.26 | convolution fusion | flops 1849999360 | bytes 27426816 | tf_op jit(solution)/shard_map/etv,ebv->etb/dot_general | solution.py:76
  163.4 13.3 %add_convert_fusion = bf16[8,160,2048]{2,1,0:T(8,128)(2,1)} fusion(f32[8,160,2048]{2,1,0:T(8,128)} %fusion.6, bf16[8,2048,352]{1,2,0:T(8,128)(2,1)} %param.22, f32[8,160,352]{2,1,0:T(8,128)} %fusion, f32[8,160,352]{2,0,1:T(8,128)S(1)} %copy-done.1), kind=kOutput, calls=%fused_computation.4 | convolution fusion | flops 1853440000 | bytes 30867456 | tf_op jit(solution)/shard_map/etv,ebv->etb/dot_general | solution.py:82
  176.8 7.7 %copy.51 = bf16[8,160,2048]{2,0,1:T(8,128)(2,1)} copy(bf16[8,160,2048]{2,1,0:T(8,128)(2,1)} %add_convert_fusion) | data formatting | bytes 10485760 | tf_op jit(solution)/shard_map/optimization_barrier | solution.py:85
  184.4 0.0 reduce-scatter.5.cloned.1.call-update
  184.4 0.0 all-gather.4.cloned.1.call-done
  184.5 4.0 %fusion.36 = f32[256,704]{0,1:T(8,128)} fusion(bf16[256,2048]{1,0:T(8,128)(2,1)} %all-gather.4.cloned.1.call-done, bf16[704,2048]{1,0:T(8,128)(2,1)} %param.28), kind=kOutput, calls=%fused_computation.73 | convolution fusion | flops 738197504 | bytes 4653056 | tf_op jit(solution)/shard_map/td,fd->tf/dot_general | solution.py:146
  188.5 47.5 %reduce-scatter.5.cloned.1.call-done = bf16[8,1,8,5,2048]{4,0,3,2,1:T(8,128)(2,1)} async-done(((bf16[8,4,8,5,2048]{4,0,3,2,1:T(8,128)(2,1)}), bf16[8,1,8,5,2048]{4,0,3,2,1:T(8,128)(2,1)}) %reduce-scatter.5.cloned.1.call-update) | async-done | bytes 1310736 | tf_op jit(solution)/shard_map/reduce_scatter | solution.py:131
  236.0 5.5 %all-to-all-start.1 = ((bf16[8,8,5,2048]{3,0,2,1:T(8,128)(2,1)}), bf16[8,8,5,2048]{3,0,2,1:T(8,128)(2,1)}, u32[]{:S(2)}, u32[]{:S(2)}) async-start(bf16[8,8,5,2048]{3,0,2,1:T(8,128)(2,1)} %bitcast.65), calls=%async_computation.3 | async-start | bytes 2621440 | tf_op jit(solution)/shard_map/all_to_all | solution.py:134
  241.5 0.2 reduce-scatter.3.cloned.1.call-start
  241.8 2.5 fusion.19
  244.3 2.0 fusion.2
  246.3 0.0 reduce-scatter.3.cloned.1.call-update
  246.4 26.4 %all-to-all-done.1 = bf16[8,8,5,2048]{3,0,2,1:T(8,128)(2,1)} async-done(((bf16[8,8,5,2048]{3,0,2,1:T(8,128)(2,1)}), bf16[8,8,5,2048]{3,0,2,1:T(8,128)(2,1)}, u32[]{:S(2)}, u32[]{:S(2)}) %all-to-all-start.1) | async-done | bytes 1310752 | tf_op jit(solution)/shard_map/all_to_all | solution.py:134
  272.8 1.6 convert_bitcast_fusion
  274.4 3.5 %copy.52 = f32[8,8,1,5,2048]{4,3,1,0,2:T(8,128)} copy(f32[8,8,1,5,2048]{4,1,3,0,2:T(8,128)S(1)} %convert_bitcast_fusion) | data formatting | bytes 5242880 | tf_op jit(solution)/shard_map/convert_element_type | solution.py:140
  277.9 4.6 %reshape.142 = f32[320,2048]{1,0:T(8,128)} reshape(f32[8,8,1,5,2048]{4,3,1,0,2:T(8,128)} %copy.52) | data formatting | bytes 5242880 | tf_op jit(solution)/shard_map/convert_element_type | solution.py:140
  282.5 5.4 %gather_fusion.1 = f32[256,2048]{1,0:T(8,128)} fusion(f32[320,2048]{1,0:T(8,128)} %reshape.142, s32[1024]{0:T(1024)S(1)} %pad_clamp_fusion.1), kind=kCustom, calls=%fused_computation.1 | custom fusion | bytes 4195328 | tf_op jit(solution)/shard_map/gather | solution.py:141
  287.8 3.5 %reshape.138 = f32[128,2,2048]{2,1,0:T(2,128)} reshape(f32[256,2048]{1,0:T(8,128)} %gather_fusion.1) | data formatting | bytes 4194304 | tf_op jit(solution)/shard_map/reshape | solution.py:142
  291.3 5.0 %reduce_sum.32 = bf16[128,2048]{1,0:T(8,128)(2,1)} reduce(f32[128,2,2048]{2,1,0:T(2,128)} %reshape.138, f32[]{:T(128)} %constant.12.clone.1), dimensions={1}, to_apply=%region_7.8 | reduce | flops 262144 | bytes 2621444 | tf_op jit(solution)/shard_map/reduce_sum | solution.py:142
  296.3 1.4 add_convert_fusion.1
  297.8 0.0 copy-start.6
  297.8 1.5 collective-permute-start
  299.3 0.0 copy-start.2
  299.3 3.9 %convolution_bitcast_fusion.1 = bf16[1,128,1024]{2,1,0:T(8,128)(2,1)S(1)} fusion(bf16[128,2048]{1,0:T(8,128)(2,1)S(1)} %add_convert_fusion.1, bf16[1024,2048]{1,0:T(8,128)(2,1)} %param.29), kind=kOutput, calls=%fused_computation.19 | convolution fusion | flops 536870912 | bytes 4980736 | tf_op jit(solution)/shard_map/td,hd->th/dot_general | solution.py:169
  303.3 7.3 %collective-permute-done = bf16[128,2048]{1,0:T(8,128)(2,1)S(1)} collective-permute-done((bf16[128,2048]{1,0:T(8,128)(2,1)S(1)}, bf16[128,2048]{1,0:T(8,128)(2,1)S(1)}, u32[]{:S(2)}, u32[]{:S(2)}) %collective-permute-start) | collective-permute-done | bytes 524320 | tf_op jit(solution)/shard_map/ppermute | solution.py:19
  310.5 1.5 convolution_bitcast_fusion
  312.0 0.1 pad_maximum_fusion
  312.1 1.4 gather_fusion.2
  (28 shorter events, 0.1 us)
Async XLA Ops:
  7.2 234.6 %copy-start = (bf16[2048,704]{0,1:T(8,128)(2,1)S(1)}, bf16[2048,704]{0,1:T(8,128)(2,1)}, u32[]{:S(2)}) copy-start(bf16[2048,704]{0,1:T(8,128)(2,1)} %param.26) | copy-start | bytes 8650756
  7.2 122.4 %all-gather.6.cloned.1.call-start = ((), (), s32[]{:S(2)}) async-start(), calls=%async_computation.7 | async-start | bytes 6553600 | tf_op jit(solution)/shard_map/all_gather | solution.py:119
  88.0 2.1 copy-start.3
  90.0 94.5 %all-gather.4.cloned.1.call-start = ((), (), s32[]{:S(2)}) async-start(), calls=%async_computation.4 | async-start | bytes 1572864 | tf_op jit(solution)/shard_map/all_gather | solution.py:145
  91.0 145.0 %reduce-scatter.5.cloned.1.call-start = ((), (), s32[]{:S(2)}) async-start(), calls=%async_computation.6 | async-start | bytes 6553600 | tf_op jit(solution)/shard_map/reduce_scatter | solution.py:131
  91.5 3.2 copy-start.7
  135.3 15.0 %copy-start.1 = (f32[8,160,352]{2,0,1:T(8,128)S(1)}, f32[8,160,352]{2,0,1:T(8,128)}, u32[]{:S(2)}) copy-start(f32[8,160,352]{2,0,1:T(8,128)} %bitcast_convert_fusion.1) | copy-start | bytes 5406724
  188.5 53.3 %copy-start.9 = (bf16[256,704]{0,1:T(8,128)(2,1)S(1)}, bf16[256,704]{0,1:T(8,128)(2,1)}, u32[]{:S(2)}) copy-start(bf16[256,704]{0,1:T(8,128)(2,1)} %param.24) | copy-start | bytes 1081348
  236.0 36.8 %all-to-all-start.1 = ((bf16[8,8,5,2048]{3,0,2,1:T(8,128)(2,1)}), bf16[8,8,5,2048]{3,0,2,1:T(8,128)(2,1)}, u32[]{:S(2)}, u32[]{:S(2)}) async-start(bf16[8,8,5,2048]{3,0,2,1:T(8,128)(2,1)} %bitcast.65), calls=%async_computation.3 | async-start | bytes 2621440 | tf_op jit(solution)/shard_map/all_to_all | solution.py:134
  241.5 54.8 %reduce-scatter.3.cloned.1.call-start = ((), (), s32[]{:S(2)}) async-start(), calls=%async_computation.5 | async-start | bytes 1572864 | tf_op jit(solution)/shard_map/reduce_scatter | solution.py:159
  241.8 2.5 copy-start.5
  241.8 2.5 copy-start.8
  291.3 5.0 %copy-start.4 = (bf16[128,2048]{1,0:T(8,128)(2,1)S(1)}, bf16[128,2048]{1,0:T(8,128)(2,1)}, u32[]{:S(2)}) copy-start(bf16[128,2048]{1,0:T(8,128)(2,1)} %param.15) | copy-start | bytes 1572868
  297.8 5.5 %copy-start.6 = (bf16[128,2048]{1,0:T(8,128)(2,1)}, bf16[128,2048]{1,0:T(8,128)(2,1)S(1)}, u32[]{:S(2)}) copy-start(bf16[128,2048]{1,0:T(8,128)(2,1)S(1)} %add_convert_fusion.1) | copy-start | bytes 1572868
  297.8 12.7 %collective-permute-start = (bf16[128,2048]{1,0:T(8,128)(2,1)S(1)}, bf16[128,2048]{1,0:T(8,128)(2,1)S(1)}, u32[]{:S(2)}, u32[]{:S(2)}) collective-permute-start(bf16[128,2048]{1,0:T(8,128)(2,1)S(1)} %add_convert_fusion.1), channel_id=1, source_target_pairs={{0,1},{1,0},{2,3},{3,2},{4,5},{5,4},{6,7},{7,6},{8,9},{9,8},{10,11... | collective-permute-start | bytes 1572872 | tf_op jit(solution)/shard_map/ppermute | solution.py:19
  299.3 11.2 %copy-start.2 = (bf16[1024,2048]{1,0:T(8,128)(2,1)S(1)}, bf16[1024,2048]{1,0:T(8,128)(2,1)}, u32[]{:S(2)}) copy-start(bf16[1024,2048]{1,0:T(8,128)(2,1)} %param.29) | copy-start | bytes 12582916
Sparse Core Ops, SparseCore 0:
  90.1 39.4 all-gather.5
  131.7 21.2 all-gather.3
  184.6 51.3 reduce-scatter.4
  246.5 26.0 reduce-scatter.2
